TPU v7x, 32 devices: a whole 2x2x4 slice. The times are simulated.
32 devices in a mesh: sim: 8 (over y, x, core), ana: 4 (over z).
Axes of the slice: x: 2, y: 2, z: 4, core: 2. Of those that a mesh axis runs over, the one named last changes fastest.
Arguments:
- initial_disp: float32 [256, 512, 128], P('ana', 'sim'), may hold values from -24 to 24
- initial_vel: float32 [256, 512, 128], P('ana', 'sim'), may hold values from -2 to 2
- stiffness: float32 [512, 128], P('sim'), may hold values from 0.05 to 0.35
- basis: float32 [512, 128, 512], P(('sim', 'ana')), may hold values from -5 to 5
- rotation: float32 [768, 512], replicated, may hold values from -0.21875 to 0.21875
Outputs:
- basis_out: float32 [512, 128, 512], P(('sim', 'ana'))
- coords: float32 [512, 256], replicated
All inputs are finite; a program needn't handle non-finite values.
Results may differ from a plain program's by a relative error of at most 0.000054.
Values sent between devices are 32-bit elements; how exact they have to be, the bound alone decides.
No kernel may reach another device: no remote copies, remote signals or barrier semaphores. Data moves between devices by JAX's collectives and lax.ppermute only.
A program may use at most 64 MiB of HBM per device.

v0:
```python
import math
import jax
import jax.numpy as jnp
from jax import lax
from jax.sharding import PartitionSpec as P

M = 256
K = 512
STEPS = 4
epsilon = 1e-06


def with_halo(value, sides, width):
    for axis, dim in sides:
        size, length = (lax.axis_size(axis), value.shape[dim])
        up = [(i, (i + 1) % size) for i in range(size - 1)]
        down = [(j, i) for i, j in up]
        last = lax.slice_in_dim(value, length - width, length, axis=dim)
        initial = lax.slice_in_dim(value, 0, width, axis=dim)
        before = lax.ppermute(last, axis, up)
        after = lax.ppermute(initial, axis, down)
        value = jnp.concatenate([before, value, after], axis=dim)
    return value


def accelerate(displace, stiffness):
    padded = with_halo(displace, (("sim", 1),), 1)
    padded = jnp.pad(padded, ((0, 0), (0, 0), (1, 1)))
    laplace = (
        padded[:, 2:, 1:-1]
        + padded[:, :-2, 1:-1]
        + padded[:, 1:-1, 2:]
        + padded[:, 1:-1, :-2]
        - 4.0 * displace
    )
    return stiffness[None] * (
        laplace - 0.5 * displace * displace * displace / (1.0 + displace * displace)
    )


def contract(left, right, left_dim, right_dim):
    return lax.dot_general(
        left,
        right,
        (((left_dim,), (right_dim,)), ((), ())),
        precision=lax.Precision.HIGHEST,
        preferred_element_type=jnp.float32,
    )


def per_device(initial_disp, initial_vel, stiffness, basis, rotation):
    displace = initial_disp
    velocity = initial_vel
    for step_index in range(STEPS):
        velocity = velocity + accelerate(displace, stiffness)
        displace = displace + velocity
    row_count = basis.shape[0] * basis.shape[1] * lax.axis_size("sim") * lax.axis_size("ana")
    basis_rows = basis.reshape(-1, K)
    totals = lax.psum(jnp.sum(displace * displace, axis=(1, 2)), "sim")
    member_scale = jnp.sqrt(totals / row_count + epsilon)
    outgoing = displace / member_scale[:, None, None]
    arrived = lax.all_to_all(outgoing, "ana", split_axis=1, concat_axis=0, tiled=True)
    unscaled = arrived.reshape(M, -1)
    coefficients = lax.psum(contract(basis_rows, unscaled, 0, 1), ("sim", "ana")) / row_count
    remainder = unscaled - contract(coefficients, basis_rows, 0, 1)
    gram_matrix = lax.psum(contract(remainder, remainder, 1, 1), ("sim", "ana")) / row_count
    factor = jnp.linalg.cholesky(gram_matrix)
    fresh_basis = jax.scipy.linalg.solve_triangular(factor, remainder, lower=True)
    top_rows = rotation[:K]
    bottom_rows = rotation[K:]
    basis_out = contract(basis_rows, top_rows, 1, 0) + contract(fresh_basis, bottom_rows, 0, 0)
    coords = (
        contract(top_rows, coefficients, 0, 0) + contract(bottom_rows, factor, 0, 1)
    ) * math.sqrt(K)
    return (basis_out.reshape(basis.shape), coords)


def solution(mesh):
    in_specs = (
        P("ana", "sim", None),
        P("ana", "sim", None),
        P("sim", None),
        P(("sim", "ana"), None, None),
        P(),
    )
    out_specs = (P(("sim", "ana"), None, None), P())
    return jax.shard_map(
        per_device, mesh=mesh, in_specs=in_specs, out_specs=out_specs, check_vma=False
    )
```

profile of v0, /device:TPU:0, one launch (start us, length us, event | category | flops | bytes accessed | tf_op | source)
XLA Modules:
  0.0 476.9 jit_solution(9723111592130537525)
XLA Ops:
  7.2 2.8 copy.23
  11.4 3.3 collective-permute-start.1
  16.7 5.5 %copy_add_fusion = (f32[64,64,128]{2,0,1:T(8,128)S(1)}, f32[64,64,128]{2,0,1:T(8,128)S(1)}) fusion(f32[64,64,128]{2,1,0:T(8,128)S(1)} %copy-done.3, f32[64,64,128]{2,0,1:T(8,128)S(1)} %copy.23, f32[64,66,130]{2,0,1:T(8,128)S(1)} %select_maximum_fusion.6, f32[64,1,128]{2,0,1:T(8,128)S(1)} %collective-permute-done.1, ...), kind=kLoop, calls=%fused_computation.118 | loop fusion | flops 8912896 | bytes 14778368 | tf_op jit(solution)/shard_map/add | solution.py:56
  23.5 5.3 %collective-permute-start.3 = (f32[64,1,128]{2,0,1:T(8,128)S(1)}, f32[64,1,128]{2,0,1:T(8,128)S(1)}, u32[]{:S(2)}, u32[]{:S(2)}) collective-permute-start(f32[64,1,128]{2,0,1:T(8,128)S(1)} %get-tuple-element.36), channel_id=1, source_target_pairs={{0,4},{4,8},{8,12},{12,16},{16,20},{20,24},{24,28},{1,5},{5,9},{9,... | collective-permute-start | bytes 98312 | tf_op jit(solution)/shard_map/ppermute | solution.py:20
  30.8 1.9 fusion.67
  34.0 5.0 %collective-permute-start.5 = (f32[64,1,128]{2,0,1:T(8,128)S(1)}, f32[64,1,128]{2,0,1:T(8,128)S(1)}, u32[]{:S(2)}, u32[]{:S(2)}) collective-permute-start(f32[64,1,128]{2,0,1:T(8,128)S(1)} %get-tuple-element.34), channel_id=1, source_target_pairs={{0,4},{4,8},{8,12},{12,16},{16,20},{20,24},{24,28},{1,5},{5,9},{9,... | collective-permute-start | bytes 98312 | tf_op jit(solution)/shard_map/ppermute | solution.py:20
  41.1 1.8 fusion.65
  44.2 5.0 %collective-permute-start.7 = (f32[64,1,128]{2,0,1:T(8,128)S(1)}, f32[64,1,128]{2,0,1:T(8,128)S(1)}, u32[]{:S(2)}, u32[]{:S(2)}) collective-permute-start(f32[64,1,128]{2,0,1:T(8,128)S(1)} %get-tuple-element.32), channel_id=1, source_target_pairs={{0,4},{4,8},{8,12},{12,16},{16,20},{20,24},{24,28},{1,5},{5,9},{9,... | collective-permute-start | bytes 98312 | tf_op jit(solution)/shard_map/ppermute | solution.py:20
  51.3 2.0 multiply_reduce_fusion
  53.3 17.1 %psum.21 = f32[64]{0:T(128)S(1)} all-reduce(f32[64]{0:T(128)S(1)} %get-tuple-element.22), channel_id=1, replica_groups=mesh['sim'=8,'ana'=4] {'sim'}, use_global_device_ids=true, to_apply=%region_1.2 | all-reduce | flops 64 | bytes 512 | tf_op jit(solution)/shard_map/psum | solution.py:59
  70.7 53.3 %all_to_all.15 = f32[64,64,128]{2,0,1:T(8,128)S(1)} all-to-all(f32[64,64,128]{2,0,1:T(8,128)S(1)} %broadcast_divide_fusion), channel_id=1, replica_groups=mesh['sim'=8,'ana'=4] {'ana'}, dimensions={1} | all-to-all | bytes 4194304 | tf_op jit(solution)/shard_map/all_to_all | solution.py:62
  126.6 4.9 %fusion.34 = f32[512,256]{0,1:T(8,128)} fusion(f32[2048,512]{1,0:T(8,128)S(1)} %bitcast.54, f32[32,8,16,128]{3,2,1,0:T(8,128)S(1)} %bitcast.55), kind=kOutput, calls=%fused_computation.71 | convolution fusion | flops 3221225472 | bytes 6815744 | tf_op jit(solution)/shard_map/dot_general | solution.py:42
  131.5 128.3 %all-reduce.8.cloned.1.call-done = f32[512,256]{0,1:T(8,128)} async-done(((f32[512,256]{0,1:T(8,128)}), f32[512,256]{0,1:T(8,128)}) %all-reduce.8.cloned.1.call-update) | async-done | bytes 524304 | tf_op jit(solution)/shard_map/psum | solution.py:64
  259.9 7.1 %convolution_subtract_fusion = f32[256,2048]{1,0:T(8,128)S(1)} fusion(f32[2048,512]{1,0:T(8,128)} %bitcast.52, f32[32,8,16,128]{3,2,1,0:T(8,128)} %bitcast.56, f32[512,256]{0,1:T(8,128)} %all-reduce.8.cloned.1.call-done), kind=kOutput, calls=%fused_computation.18 | convolution fusion | flops 3221880832 | bytes 8912896 | tf_op jit(solution)/shard_map/dot_general | solution.py:42
  267.0 2.6 fusion.75
  269.6 10.3 %fusion.40 = f32[2048,512]{1,0:T(8,128)} fusion(f32[2048,512]{1,0:T(8,128)} %bitcast.53, f32[768,512]{1,0:T(8,128)} %param.9), kind=kOutput, calls=%fused_computation.77 | convolution fusion | flops 6442450944 | bytes 9437184 | tf_op jit(solution)/shard_map/dot_general | solution.py:42
  279.9 113.8 %all-reduce.10.cloned.1.call-done = f32[256,256]{0,1:T(8,128)} async-done(((f32[256,256]{0,1:T(8,128)}), f32[256,256]{0,1:T(8,128)}) %all-reduce.10.cloned.1.call-update) | async-done | bytes 262160 | tf_op jit(solution)/shard_map/psum | solution.py:66
  395.8 11.7 %cholesky.50 = f32[128,128]{1,0:T(8,128)S(1)} custom-call(f32[128,128]{1,0:T(8,128)S(1)} %cholesky.118), custom_call_target="Cholesky" | custom-call | tf_op jit(solution)/shard_map/jit(cholesky)/cholesky | solution.py:67
  407.6 9.8 %custom-call.15 = f32[1,128,128]{1,2,0:T(8,128)S(1)} custom-call(f32[1,128,128]{2,1,0:T(8,128)S(1)} %get-tuple-element.43), custom_call_target="InvertDiagBlocksLowerTriangular" | custom-call | tf_op jit(solution)/shard_map/jit(cholesky)/cholesky | solution.py:67
  417.9 11.7 %cholesky.105 = f32[128,128]{1,0:T(8,128)S(1)} custom-call(f32[128,128]{1,0:T(8,128)S(1)} %convolution_subtract_fusion.2), custom_call_target="Cholesky" | custom-call | tf_op jit(solution)/shard_map/jit(cholesky)/cholesky | solution.py:67
  431.7 1.8 fusion.42
  436.3 4.0 while.1
  440.4 19.7 %custom-call.16 = f32[2,128,128]{1,2,0:T(8,128)S(1)} custom-call(f32[2,128,128]{2,1,0:T(8,128)S(1)} %get-tuple-element.9), custom_call_target="InvertDiagBlocksLowerTriangular" | custom-call | tf_op jit(solution)/shard_map/jit(_solve_triangular)/triangular_solve | solution.py:68
  463.3 6.3 %convolution_add_fusion = f32[2048,512]{1,0:T(8,128)} fusion(f32[2048,512]{1,0:T(8,128)S(1)} %copy-done.1, f32[128,2048]{1,0:T(8,128)S(1)} %fusion.55, f32[128,2048]{1,0:T(8,128)S(1)} %fusion.37, f32[768,512]{1,0:T(8,128)} %param.9), kind=kOutput, calls=%fused_computation.13 | convolution fusion | flops 3222798336 | bytes 11010048 | tf_op jit(solution)/shard_map/dot_general | solution.py:42
  (70 shorter events, 29.5 us)
Async XLA Ops:
  7.2 252.7 %all-reduce.8.cloned.1.call-start = ((), (), s32[]{:S(2)}) async-start(), calls=%async_computation.1 | async-start | bytes 1048576 | tf_op jit(solution)/shard_map/psum | solution.py:64
  10.0 4.6 collective-permute-start
  11.3 5.4 %copy-start.3 = (f32[64,64,128]{2,1,0:T(8,128)S(1)}, f32[64,64,128]{2,1,0:T(8,128)}, u32[]{:S(2)}) copy-start(f32[64,64,128]{2,1,0:T(8,128)} %param.5) | copy-start | bytes 6291460
  11.3 5.4 %copy-start.5 = (f32[64,64,128]{2,1,0:T(8,128)S(1)}, f32[64,64,128]{2,1,0:T(8,128)}, u32[]{:S(2)}) copy-start(f32[64,64,128]{2,1,0:T(8,128)} %param.6) | copy-start | bytes 6291460
  11.4 5.4 %copy-start.8 = (f32[64,128]{1,0:T(8,128)S(1)}, f32[64,128]{1,0:T(8,128)}, u32[]{:S(2)}) copy-start(f32[64,128]{1,0:T(8,128)} %param.7) | copy-start | bytes 98308
  11.4 4.1 collective-permute-start.1
  22.2 6.6 %collective-permute-start.2 = (f32[64,1,128]{2,0,1:T(8,128)S(1)}, f32[64,1,128]{2,0,1:T(8,128)S(1)}, u32[]{:S(2)}, u32[]{:S(2)}) collective-permute-start(f32[64,1,128]{2,0,1:T(8,128)S(1)} %get-tuple-element.37), channel_id=1, source_target_pairs={{4,0},{8,4},{12,8},{16,12},{20,16},{24,20},{28,24},{5,1},{9,5},{13... | collective-permute-start | bytes 98312 | tf_op jit(solution)/shard_map/ppermute | solution.py:21
  23.5 6.1 %collective-permute-start.3 = (f32[64,1,128]{2,0,1:T(8,128)S(1)}, f32[64,1,128]{2,0,1:T(8,128)S(1)}, u32[]{:S(2)}, u32[]{:S(2)}) collective-permute-start(f32[64,1,128]{2,0,1:T(8,128)S(1)} %get-tuple-element.36), channel_id=1, source_target_pairs={{0,4},{4,8},{8,12},{12,16},{16,20},{20,24},{24,28},{1,5},{5,9},{9,... | collective-permute-start | bytes 98312 | tf_op jit(solution)/shard_map/ppermute | solution.py:20
  32.7 6.3 %collective-permute-start.4 = (f32[64,1,128]{2,0,1:T(8,128)S(1)}, f32[64,1,128]{2,0,1:T(8,128)S(1)}, u32[]{:S(2)}, u32[]{:S(2)}) collective-permute-start(f32[64,1,128]{2,0,1:T(8,128)S(1)} %get-tuple-element.35), channel_id=1, source_target_pairs={{4,0},{8,4},{12,8},{16,12},{20,16},{24,20},{28,24},{5,1},{9,5},{13... | collective-permute-start | bytes 98312 | tf_op jit(solution)/shard_map/ppermute | solution.py:21
  34.0 5.9 %collective-permute-start.5 = (f32[64,1,128]{2,0,1:T(8,128)S(1)}, f32[64,1,128]{2,0,1:T(8,128)S(1)}, u32[]{:S(2)}, u32[]{:S(2)}) collective-permute-start(f32[64,1,128]{2,0,1:T(8,128)S(1)} %get-tuple-element.34), channel_id=1, source_target_pairs={{0,4},{4,8},{8,12},{12,16},{16,20},{20,24},{24,28},{1,5},{5,9},{9,... | collective-permute-start | bytes 98312 | tf_op jit(solution)/shard_map/ppermute | solution.py:20
  42.9 6.3 %collective-permute-start.6 = (f32[64,1,128]{2,0,1:T(8,128)S(1)}, f32[64,1,128]{2,0,1:T(8,128)S(1)}, u32[]{:S(2)}, u32[]{:S(2)}) collective-permute-start(f32[64,1,128]{2,0,1:T(8,128)S(1)} %get-tuple-element.33), channel_id=1, source_target_pairs={{4,0},{8,4},{12,8},{16,12},{20,16},{24,20},{28,24},{5,1},{9,5},{13... | collective-permute-start | bytes 98312 | tf_op jit(solution)/shard_map/ppermute | solution.py:21
  44.2 5.9 %collective-permute-start.7 = (f32[64,1,128]{2,0,1:T(8,128)S(1)}, f32[64,1,128]{2,0,1:T(8,128)S(1)}, u32[]{:S(2)}, u32[]{:S(2)}) collective-permute-start(f32[64,1,128]{2,0,1:T(8,128)S(1)} %get-tuple-element.32), channel_id=1, source_target_pairs={{0,4},{4,8},{8,12},{12,16},{16,20},{20,24},{24,28},{1,5},{5,9},{9,... | collective-permute-start | bytes 98312 | tf_op jit(solution)/shard_map/ppermute | solution.py:20
  124.0 2.5 copy-start
  125.3 1.3 copy-start.2
  131.5 262.1 %all-reduce.10.cloned.1.call-start = ((), (), s32[]{:S(2)}) async-start(), calls=%async_computation.2 | async-start | bytes 524288 | tf_op jit(solution)/shard_map/psum | solution.py:66
  394.6 39.6 %copy-start.6 = (f32[512,256]{0,1:T(8,128)S(1)}, f32[512,256]{0,1:T(8,128)}, u32[]{:S(2)}) copy-start(f32[512,256]{0,1:T(8,128)} %all-reduce.8.cloned.1.call-done) | copy-start | bytes 1572868
  431.6 2.6 copy-start.4
  434.2 2.1 copy-start.7
  461.1 2.2 copy-start.1
Sparse Core Ops, SparseCore 0:
  131.6 128.2 all-reduce.7
  269.7 123.9 all-reduce.9
where the time goes:
time: 486 us; the launch traced here: 477 us
  waiting for transfers between devices  245 us (50%)
  other arithmetic  72.6 us (15%)
  blocking collectives  70.4 us (14%)
  matrix products  37.5 us (8%)
  starting transfers between devices  23.8 us (5%)
  between operations  16.2 us (3%)
  local copies, waits for them, and re-layouts  10.5 us (2%)
    psum x1, waiting for transfers between devices, per_device(): lax.psum(contract(basis_rows, unscaled, 0, 1), ('sim', 'ana')) / row_count  128 us
    psum x1, waiting for transfers between devices, per_device(): lax.psum(contract(remainder, remainder, 1, 1), ('sim', 'ana')) / row_count  114 us
    all_to_all x1, blocking collectives, per_device(): lax.all_to_all(outgoing, 'ana', split_axis=1, concat_axis=0, tiled=True)  53.3 us
    another operation x6, other arithmetic, per_device(): factor = jnp.linalg.cholesky(gram_matrix)  34 us
    dot_general x7, matrix products, contract(): lax.dot_general(left, right, (((left_dim,), (right_dim,)), ((), ())), pre...  33.9 us
    another operation x3, other arithmetic, per_device(): jax.scipy.linalg.solve_triangular(factor, remainder, lower=True)  20.4 us
    ppermute x4, starting transfers between devices, with_halo(): before = lax.ppermute(last, axis, up)  18.6 us
    psum x1, blocking collectives, per_device(): totals = lax.psum(jnp.sum(displace * displace, axis=(1, 2)), 'sim')  17.1 us
  transfers between devices with their start and end apart: 10, of which 6 were waited for; matrix products, arithmetic and copies ran while one was open for 2% of the time, Pallas kernels for 0%

commit v1 on v0

--- a/solution.py
+++ b/solution.py
@@ -8,6 +8,28 @@
 K = 512
 STEPS = 4
 epsilon = 1e-06
+
+
+def split_up(x, dim, peers):
+    before, after = (x.shape[:dim], x.shape[dim + 1 :])
+    return jnp.moveaxis(x.reshape(*before, peers, -1, *after), dim, 0)
+
+
+def laid_out(pieces, dim):
+    dims = list(pieces.shape[1:])
+    dims[dim] *= pieces.shape[0]
+    return jnp.moveaxis(pieces, 0, dim).reshape(dims)
+
+
+def swapped_with_each(value, axis, split_dim, concat_dim):
+    peers, position = (lax.axis_size(axis), lax.axis_index(axis))
+    tiles = split_up(value, split_dim, peers)
+    outs = [tiles[position]]
+    for step in range(1, peers):
+        sent = tiles[position ^ step]
+        outs.append(lax.ppermute(sent, axis, [(i, i ^ step) for i in range(peers)]))
+    tiles = jnp.stack(outs)[position ^ jnp.arange(peers)]
+    return laid_out(tiles, concat_dim)
 
 
 def with_halo(value, sides, width):
@@ -59,7 +81,7 @@
     totals = lax.psum(jnp.sum(displace * displace, axis=(1, 2)), "sim")
     member_scale = jnp.sqrt(totals / row_count + epsilon)
     outgoing = displace / member_scale[:, None, None]
-    arrived = lax.all_to_all(outgoing, "ana", split_axis=1, concat_axis=0, tiled=True)
+    arrived = swapped_with_each(outgoing, "ana", 1, 0)
     unscaled = arrived.reshape(M, -1)
     coefficients = lax.psum(contract(basis_rows, unscaled, 0, 1), ("sim", "ana")) / row_count
     remainder = unscaled - contract(coefficients, basis_rows, 0, 1)

time: 486 us -> 490 us (level)
  blocking collectives: 70.4 us -> 17.1 us
  waiting for transfers between devices: 245 us -> 291 us
  other arithmetic: 72.6 us -> 78.5 us
    all_to_all x1 -> x0, blocking collectives: 53.3 us -> none  [per_device(): lax.all_to_all(outgoing, 'ana', split_axis=1, concat_axis=0, tiled=True)]
    ppermute x0 -> x3, waiting for transfers between devices: none -> 35.4 us  [swapped_with_each(): outs.append(lax.ppermute(sent, axis, [(i, i ^ step) for i in range(peers)]))]
    psum x1, waiting for transfers between devices: 128 us -> 138 us  [per_device(): lax.psum(contract(basis_rows, unscaled, 0, 1), ('sim', 'ana')) / row_count]
  transfers between devices with their start and end apart: 10 -> 13, of which waited for: 6 -> 8; matrix products, arithmetic and copies ran while one was open for 2% -> 2% of each run, Pallas kernels for 0% -> 0%
where the time goes in v1:
time: 490 us; the launch traced here: 481 us
  waiting for transfers between devices  291 us (59%)
  other arithmetic  78.5 us (16%)
  matrix products  40.4 us (8%)
  starting transfers between devices  28.5 us (6%)
  blocking collectives  17.1 us (3%)
  between operations  16.3 us (3%)
  local copies, waits for them, and re-layouts  8.96 us (2%)
    psum x1, waiting for transfers between devices, per_device(): lax.psum(contract(basis_rows, unscaled, 0, 1), ('sim', 'ana')) / row_count  138 us
    psum x1, waiting for transfers between devices, per_device(): lax.psum(contract(remainder, remainder, 1, 1), ('sim', 'ana')) / row_count  114 us
    dot_general x7, matrix products, contract(): lax.dot_general(left, right, (((left_dim,), (right_dim,)), ((), ())), pre...  36.9 us
    ppermute x3, waiting for transfers between devices, swapped_with_each(): outs.append(lax.ppermute(sent, axis, [(i, i ^ step) for i in range(peers)]))  35.4 us
    another operation x6, other arithmetic, per_device(): factor = jnp.linalg.cholesky(gram_matrix)  34 us
    another operation x3, other arithmetic, per_device(): jax.scipy.linalg.solve_triangular(factor, remainder, lower=True)  20.4 us
    ppermute x4, starting transfers between devices, with_halo(): before = lax.ppermute(last, axis, up)  18.6 us
    psum x1, blocking collectives, per_device(): totals = lax.psum(jnp.sum(displace * displace, axis=(1, 2)), 'sim')  17.1 us
  transfers between devices with their start and end apart: 13, of which 8 were waited for; matrix products, arithmetic and copies ran while one was open for 2% of the time, Pallas kernels for 0%

profile of v1, /device:TPU:0, one launch (start us, length us, event | category | flops | bytes accessed | tf_op | source)
XLA Modules:
  0.0 481.0 jit_solution(5185057669884467563)
XLA Ops:
  9.6 3.3 collective-permute-start.1
  13.8 3.2 select_maximum_fusion.6
  20.5 5.3 %collective-permute-start.3 = (f32[64,1,128]{2,1,0:T(1,128)S(1)}, f32[64,1,128]{2,1,0:T(1,128)S(1)}, u32[]{:S(2)}, u32[]{:S(2)}) collective-permute-start(f32[64,1,128]{2,1,0:T(1,128)S(1)} %get-tuple-element.38), channel_id=1, source_target_pairs={{0,4},{4,8},{8,12},{12,16},{16,20},{20,24},{24,28},{1,5},{5,9},{9,... | collective-permute-start | bytes 98312 | tf_op jit(solution)/shard_map/ppermute | solution.py:42
  31.8 5.0 %collective-permute-start.5 = (f32[64,1,128]{2,1,0:T(1,128)S(1)}, f32[64,1,128]{2,1,0:T(1,128)S(1)}, u32[]{:S(2)}, u32[]{:S(2)}) collective-permute-start(f32[64,1,128]{2,1,0:T(1,128)S(1)} %get-tuple-element.36), channel_id=1, source_target_pairs={{0,4},{4,8},{8,12},{12,16},{16,20},{20,24},{24,28},{1,5},{5,9},{9,... | collective-permute-start | bytes 98312 | tf_op jit(solution)/shard_map/ppermute | solution.py:42
  39.3 3.2 fusion.66
  43.8 5.0 %collective-permute-start.7 = (f32[64,1,128]{2,1,0:T(1,128)S(1)}, f32[64,1,128]{2,1,0:T(1,128)S(1)}, u32[]{:S(2)}, u32[]{:S(2)}) collective-permute-start(f32[64,1,128]{2,1,0:T(1,128)S(1)} %get-tuple-element.34), channel_id=1, source_target_pairs={{0,4},{4,8},{8,12},{12,16},{16,20},{20,24},{24,28},{1,5},{5,9},{9,... | collective-permute-start | bytes 98312 | tf_op jit(solution)/shard_map/ppermute | solution.py:42
  51.2 3.3 multiply_reduce_fusion
  54.5 17.1 %psum.21 = f32[64]{0:T(128)S(1)} all-reduce(f32[64]{0:T(128)S(1)} %get-tuple-element.20), channel_id=1, replica_groups=mesh['sim'=8,'ana'=4] {'sim'}, use_global_device_ids=true, to_apply=%region_1.2 | all-reduce | flops 64 | bytes 512 | tf_op jit(solution)/shard_map/psum | solution.py:81
  75.4 2.6 collective-permute-start.9
  78.2 20.4 %collective-permute-done.8 = f32[64,16,128]{2,1,0:T(8,128)S(1)} collective-permute-done((f32[64,16,128]{2,1,0:T(8,128)S(1)}, f32[64,16,128]{2,1,0:T(8,128)S(1)}, u32[]{:S(2)}, u32[]{:S(2)}) %collective-permute-start.8) | collective-permute-done | bytes 524320 | tf_op jit(solution)/shard_map/ppermute | solution.py:30
  98.6 15.0 %collective-permute-done.9 = f32[64,16,128]{2,1,0:T(8,128)S(1)} collective-permute-done((f32[64,16,128]{2,1,0:T(8,128)S(1)}, f32[64,16,128]{2,1,0:T(8,128)S(1)}, u32[]{:S(2)}, u32[]{:S(2)}) %collective-permute-start.9) | collective-permute-done | bytes 524320 | tf_op jit(solution)/shard_map/ppermute | solution.py:30
  115.1 2.3 gather_fusion
  117.4 7.8 %fusion.34 = f32[512,256]{0,1:T(8,128)} fusion(f32[2048,512]{1,0:T(8,128)} %bitcast.64, f32[32,8,16,128]{3,2,1,0:T(8,128)S(1)} %bitcast.67), kind=kOutput, calls=%fused_computation.73 | convolution fusion | flops 3221225472 | bytes 6815744 | tf_op jit(solution)/shard_map/dot_general | solution.py:64
  125.5 138.4 %all-reduce.8.cloned.1.call-done = f32[512,256]{0,1:T(8,128)} async-done(((f32[512,256]{0,1:T(8,128)}), f32[512,256]{0,1:T(8,128)}) %all-reduce.8.cloned.1.call-update) | async-done | bytes 524304 | tf_op jit(solution)/shard_map/psum | solution.py:86
  263.9 7.1 %convolution_subtract_fusion = f32[256,2048]{1,0:T(8,128)S(1)} fusion(f32[2048,512]{1,0:T(8,128)} %bitcast.65, f32[32,8,16,128]{3,2,1,0:T(8,128)} %bitcast.68, f32[512,256]{0,1:T(8,128)} %all-reduce.8.cloned.1.call-done), kind=kOutput, calls=%fused_computation.19 | convolution fusion | flops 3221880832 | bytes 8912896 | tf_op jit(solution)/shard_map/dot_general | solution.py:64
  271.0 2.6 fusion.77
  273.6 10.3 %fusion.40 = f32[2048,512]{1,0:T(8,128)} fusion(f32[2048,512]{1,0:T(8,128)} %bitcast.66, f32[768,512]{1,0:T(8,128)} %param.9), kind=kOutput, calls=%fused_computation.79 | convolution fusion | flops 6442450944 | bytes 9437184 | tf_op jit(solution)/shard_map/dot_general | solution.py:64
  283.9 113.7 %all-reduce.10.cloned.1.call-done = f32[256,256]{0,1:T(8,128)} async-done(((f32[256,256]{0,1:T(8,128)}), f32[256,256]{0,1:T(8,128)}) %all-reduce.10.cloned.1.call-update) | async-done | bytes 262160 | tf_op jit(solution)/shard_map/psum | solution.py:88
  399.8 11.7 %cholesky.50 = f32[128,128]{1,0:T(8,128)S(1)} custom-call(f32[128,128]{1,0:T(8,128)S(1)} %cholesky.118), custom_call_target="Cholesky" | custom-call | tf_op jit(solution)/shard_map/jit(cholesky)/cholesky | solution.py:89
  411.6 9.8 %custom-call.15 = f32[1,128,128]{1,2,0:T(8,128)S(1)} custom-call(f32[1,128,128]{2,1,0:T(8,128)S(1)} %get-tuple-element.45), custom_call_target="InvertDiagBlocksLowerTriangular" | custom-call | tf_op jit(solution)/shard_map/jit(cholesky)/cholesky | solution.py:89
  421.9 11.7 %cholesky.105 = f32[128,128]{1,0:T(8,128)S(1)} custom-call(f32[128,128]{1,0:T(8,128)S(1)} %convolution_subtract_fusion.2), custom_call_target="Cholesky" | custom-call | tf_op jit(solution)/shard_map/jit(cholesky)/cholesky | solution.py:89
  440.3 4.2 while.1
  444.5 19.7 %custom-call.16 = f32[2,128,128]{1,2,0:T(8,128)S(1)} custom-call(f32[2,128,128]{2,1,0:T(8,128)S(1)} %get-tuple-element.9), custom_call_target="InvertDiagBlocksLowerTriangular" | custom-call | tf_op jit(solution)/shard_map/jit(_solve_triangular)/triangular_solve | solution.py:90
  467.4 6.2 %convolution_add_fusion = f32[2048,512]{1,0:T(8,128)} fusion(f32[2048,512]{1,0:T(8,128)S(1)} %copy-done, f32[128,2048]{1,0:T(8,128)S(1)} %fusion.55, f32[128,2048]{1,0:T(8,128)S(1)} %fusion.37, f32[768,512]{1,0:T(8,128)} %param.9), kind=kOutput, calls=%fused_computation.14 | convolution fusion | flops 3222798336 | bytes 11010048 | tf_op jit(solution)/shard_map/dot_general | solution.py:64
  (78 shorter events, 39.8 us)
Async XLA Ops:
  7.2 256.7 %all-reduce.8.cloned.1.call-start = ((), (), s32[]{:S(2)}) async-start(), calls=%async_computation | async-start | bytes 1048576 | tf_op jit(solution)/shard_map/psum | solution.py:86
  8.3 4.6 collective-permute-start
  9.6 7.4 %copy-start.2 = (f32[64,64,128]{2,1,0:T(8,128)S(1)}, f32[64,64,128]{2,1,0:T(8,128)}, u32[]{:S(2)}) copy-start(f32[64,64,128]{2,1,0:T(8,128)} %param.5) | copy-start | bytes 6291460
  9.6 7.4 %copy-start.6 = (f32[64,64,128]{2,1,0:T(8,128)S(1)}, f32[64,64,128]{2,1,0:T(8,128)}, u32[]{:S(2)}) copy-start(f32[64,64,128]{2,1,0:T(8,128)} %param.6) | copy-start | bytes 6291460
  9.6 7.3 %copy-start.8 = (f32[64,128]{1,0:T(8,128)S(1)}, f32[64,128]{1,0:T(8,128)}, u32[]{:S(2)}) copy-start(f32[64,128]{1,0:T(8,128)} %param.7) | copy-start | bytes 98308
  9.6 4.1 collective-permute-start.1
  19.2 6.6 %collective-permute-start.2 = (f32[64,1,128]{2,1,0:T(1,128)S(1)}, f32[64,1,128]{2,1,0:T(1,128)S(1)}, u32[]{:S(2)}, u32[]{:S(2)}) collective-permute-start(f32[64,1,128]{2,1,0:T(1,128)S(1)} %get-tuple-element.39), channel_id=1, source_target_pairs={{4,0},{8,4},{12,8},{16,12},{20,16},{24,20},{28,24},{5,1},{9,5},{13... | collective-permute-start | bytes 98312 | tf_op jit(solution)/shard_map/ppermute | solution.py:43
  20.5 6.1 %collective-permute-start.3 = (f32[64,1,128]{2,1,0:T(1,128)S(1)}, f32[64,1,128]{2,1,0:T(1,128)S(1)}, u32[]{:S(2)}, u32[]{:S(2)}) collective-permute-start(f32[64,1,128]{2,1,0:T(1,128)S(1)} %get-tuple-element.38), channel_id=1, source_target_pairs={{0,4},{4,8},{8,12},{12,16},{16,20},{20,24},{24,28},{1,5},{5,9},{9,... | collective-permute-start | bytes 98312 | tf_op jit(solution)/shard_map/ppermute | solution.py:42
  30.5 6.3 %collective-permute-start.4 = (f32[64,1,128]{2,1,0:T(1,128)S(1)}, f32[64,1,128]{2,1,0:T(1,128)S(1)}, u32[]{:S(2)}, u32[]{:S(2)}) collective-permute-start(f32[64,1,128]{2,1,0:T(1,128)S(1)} %get-tuple-element.37), channel_id=1, source_target_pairs={{4,0},{8,4},{12,8},{16,12},{20,16},{24,20},{28,24},{5,1},{9,5},{13... | collective-permute-start | bytes 98312 | tf_op jit(solution)/shard_map/ppermute | solution.py:43
  31.8 5.9 %collective-permute-start.5 = (f32[64,1,128]{2,1,0:T(1,128)S(1)}, f32[64,1,128]{2,1,0:T(1,128)S(1)}, u32[]{:S(2)}, u32[]{:S(2)}) collective-permute-start(f32[64,1,128]{2,1,0:T(1,128)S(1)} %get-tuple-element.36), channel_id=1, source_target_pairs={{0,4},{4,8},{8,12},{12,16},{16,20},{20,24},{24,28},{1,5},{5,9},{9,... | collective-permute-start | bytes 98312 | tf_op jit(solution)/shard_map/ppermute | solution.py:42
  42.5 6.4 %collective-permute-start.6 = (f32[64,1,128]{2,1,0:T(1,128)S(1)}, f32[64,1,128]{2,1,0:T(1,128)S(1)}, u32[]{:S(2)}, u32[]{:S(2)}) collective-permute-start(f32[64,1,128]{2,1,0:T(1,128)S(1)} %get-tuple-element.35), channel_id=1, source_target_pairs={{4,0},{8,4},{12,8},{16,12},{20,16},{24,20},{28,24},{5,1},{9,5},{13... | collective-permute-start | bytes 98312 | tf_op jit(solution)/shard_map/ppermute | solution.py:43
  43.8 5.9 %collective-permute-start.7 = (f32[64,1,128]{2,1,0:T(1,128)S(1)}, f32[64,1,128]{2,1,0:T(1,128)S(1)}, u32[]{:S(2)}, u32[]{:S(2)}) collective-permute-start(f32[64,1,128]{2,1,0:T(1,128)S(1)} %get-tuple-element.34), channel_id=1, source_target_pairs={{0,4},{4,8},{8,12},{12,16},{16,20},{20,24},{24,28},{1,5},{5,9},{9,... | collective-permute-start | bytes 98312 | tf_op jit(solution)/shard_map/ppermute | solution.py:42
  48.8 2.4 copy-start.3
  73.8 24.9 %collective-permute-start.8 = (f32[64,16,128]{2,1,0:T(8,128)S(1)}, f32[64,16,128]{2,1,0:T(8,128)S(1)}, u32[]{:S(2)}, u32[]{:S(2)}) collective-permute-start(f32[64,16,128]{2,1,0:T(8,128)S(1)} %get-tuple-element.33), channel_id=1, source_target_pairs={{0,1},{1,0},{2,3},{3,2},{4,5},{5,4},{6,7},{7,6},{8,9},{9,8},{10,11... | collective-permute-start | bytes 1572872 | tf_op jit(solution)/shard_map/ppermute | solution.py:30
  75.4 38.2 %collective-permute-start.9 = (f32[64,16,128]{2,1,0:T(8,128)S(1)}, f32[64,16,128]{2,1,0:T(8,128)S(1)}, u32[]{:S(2)}, u32[]{:S(2)}) collective-permute-start(f32[64,16,128]{2,1,0:T(8,128)S(1)} %get-tuple-element.32), channel_id=1, source_target_pairs={{0,2},{1,3},{2,0},{3,1},{4,6},{5,7},{6,4},{7,5},{8,10},{9,11},{10,... | collective-permute-start | bytes 1572872 | tf_op jit(solution)/shard_map/ppermute | solution.py:30
  78.0 35.6 %collective-permute-start.10 = (f32[64,16,128]{2,1,0:T(8,128)S(1)}, f32[64,16,128]{2,1,0:T(8,128)S(1)}, u32[]{:S(2)}, u32[]{:S(2)}) collective-permute-start(f32[64,16,128]{2,1,0:T(8,128)S(1)} %get-tuple-element.31), channel_id=1, source_target_pairs={{0,3},{1,2},{2,1},{3,0},{4,7},{5,6},{6,5},{7,4},{8,11},{9,10},{10,... | collective-permute-start | bytes 1572872 | tf_op jit(solution)/shard_map/ppermute | solution.py:30
  117.4 7.8 %copy-start.1 = (f32[4,64,16,128]{3,2,1,0:T(8,128)}, f32[4,64,16,128]{3,2,1,0:T(8,128)S(1)}, u32[]{:S(2)}) copy-start(f32[4,64,16,128]{3,2,1,0:T(8,128)S(1)} %gather_fusion) | copy-start | bytes 6291460
  125.2 272.4 %all-reduce.10.cloned.1.call-start = ((), (), s32[]{:S(2)}) async-start(), calls=%async_computation.1 | async-start | bytes 524288 | tf_op jit(solution)/shard_map/psum | solution.py:88
  398.6 39.5 %copy-start.5 = (f32[512,256]{0,1:T(8,128)S(1)}, f32[512,256]{0,1:T(8,128)}, u32[]{:S(2)}) copy-start(f32[512,256]{0,1:T(8,128)} %all-reduce.8.cloned.1.call-done) | copy-start | bytes 1572868
  435.6 2.6 copy-start.4
  438.2 2.1 copy-start.7
  465.2 2.2 copy-start
Sparse Core Ops, SparseCore 0:
  125.4 138.4 all-reduce.7
  273.7 123.9 all-reduce.9
